TPU v7x, 512 devices: a whole 4x8x8 slice. The times are simulated.
512 devices in a mesh: dp: 4 (over y_hi), seq: 128 (over y_lo, x, z, core).
Axes of the slice: x: 4, y: 8 (y_hi: 4, y_lo: 2; y = y_hi * 2 + y_lo), z: 8, core: 2. Of those that a mesh axis runs over, the one named last changes fastest.
Arguments:
- queries: bfloat16 [4, 16384, 512], P('dp', 'seq'), may hold values from -6 to 6
- key_rows: bfloat16 [4, 16384, 512], P('dp', 'seq'), may hold values from -6 to 6
- value_rows: bfloat16 [4, 16384, 512], P('dp', 'seq'), may hold values from -6 to 6
- out_grad: bfloat16 [4, 16384, 1024], P('dp', 'seq'), may hold values from -6 to 6
- out_weight: bfloat16 [512, 1024], P('seq'), may hold values from -0.25 to 0.25
- norm_gain: float32 [256], replicated, may hold values from 0.1 to 1.9
Outputs:
- query_grad: bfloat16 [4, 16384, 512], P('dp', 'seq')
- key_grad: bfloat16 [4, 16384, 512], P('dp', 'seq')
- value_grad: bfloat16 [4, 16384, 512], P('dp', 'seq')
- weight_grad: float32 [512, 1024], P('seq')
All inputs are finite; a program needn't handle non-finite values.
Results may differ from a plain program's by a relative error of at most 0.025.
Values may be sent and summed in bfloat16 or wider, within the bound.
A program may use at most 64 MiB of HBM per device.

v0:
```python
import math
import jax
import jax.numpy as jnp
from jax import lax
from jax.sharding import PartitionSpec as P

DH = 128
SOFT_HEADS = 2
LIN_HEADS = 2
WINDOW = 256
HALF = 128
norm_eps = 1e-06


def with_halo(block, sides, width):
    for axis, dim in sides:
        count = lax.axis_size(axis)
        forward = [(i, i + 1) for i in range(count - 1)]
        forward.append((count - 1, 0))
        backward = [(target, source) for source, target in forward]
        low = lax.ppermute(
            lax.slice_in_dim(block, block.shape[dim] - width, None, axis=dim), axis, forward
        )
        high = lax.ppermute(lax.slice_in_dim(block, 0, width, axis=dim), axis, backward)
        block = jnp.concatenate([low, block, high], axis=dim)
    return block


def from_behind(value, axis, steps):
    count = lax.axis_size(axis)
    pairs = [(source, (source + steps) % count) for source in range(count)]
    return lax.ppermute(value, axis, pairs)


def unit_plus(values):
    return jnp.where(values > 0, values + 1.0, jnp.exp(jnp.minimum(values, 0.0)))


def unit_slope(values):
    return jnp.where(values > 0, 1.0, jnp.exp(jnp.minimum(values, 0.0)))


def body(queries, key_rows, value_rows, out_grad, out_weight, norm_gain):
    highest = lax.Precision.HIGHEST
    query_all = queries[0]
    key_all = key_rows[0]
    value_all = value_rows[0]
    grad_out = out_grad[0]
    tok_rows = query_all.shape[0]
    soft = SOFT_HEADS * DH
    factor = DH ** (-0.5)
    span_rows = tok_rows + 2 * HALF
    key_value = jnp.stack([key_all[:, :soft], value_all[:, :soft]])
    padded = with_halo(key_value, (("seq", 1),), HALF)
    query_soft = query_all[:, :soft].reshape(tok_rows, SOFT_HEADS, DH)
    key_soft = padded[0].reshape(span_rows, SOFT_HEADS, DH)
    value_soft = padded[1].reshape(span_rows, SOFT_HEADS, DH)
    scores = (
        jnp.einsum("ihd,jhd->hij", query_soft, key_soft, preferred_element_type=jnp.float32)
        * factor
    )
    row_pos = lax.broadcasted_iota(jnp.int32, (tok_rows, span_rows), 0)
    col_pos = lax.broadcasted_iota(jnp.int32, (tok_rows, span_rows), 1)
    inside = (col_pos >= row_pos) & (col_pos < row_pos + WINDOW)
    scores = jnp.where(inside, scores, -1e30)
    row_peak = jnp.max(scores, axis=2, keepdims=True)
    exp_terms = jnp.where(inside, jnp.exp(scores - row_peak), 0.0)
    attn_probs = exp_terms / jnp.sum(exp_terms, axis=2, keepdims=True)
    probs_low = attn_probs.astype(jnp.bfloat16)
    attn_soft = jnp.einsum(
        "hij,jhd->ihd", probs_low, value_soft, preferred_element_type=jnp.float32
    ).astype(jnp.bfloat16)
    query_lin = query_all[:, soft:].astype(jnp.float32).reshape(tok_rows, LIN_HEADS, DH)
    key_lin = key_all[:, soft:].astype(jnp.float32).reshape(tok_rows, LIN_HEADS, DH)
    value_lin = value_all[:, soft:].astype(jnp.float32).reshape(tok_rows, LIN_HEADS, DH)
    phi_query = unit_plus(query_lin)
    phi_key = unit_plus(key_lin)
    state_term = jnp.einsum("jha,jhb->hab", phi_key, value_lin, precision=highest)
    lin_state = lax.psum(state_term, "seq")
    lin_u = jnp.einsum("iha,hab->ihb", phi_query, lin_state, precision=highest)
    lin_r = lax.rsqrt(jnp.mean(lin_u * lin_u, axis=2, keepdims=True) + norm_eps)
    gain_heads = norm_gain.reshape(LIN_HEADS, DH)
    attn_lin = (gain_heads * lin_u * lin_r).astype(jnp.bfloat16)
    attn = jnp.concatenate(
        [attn_soft.reshape(tok_rows, soft), attn_lin.reshape(tok_rows, LIN_HEADS * DH)], axis=1
    )
    d_attn = lax.dot_general(
        grad_out,
        lax.all_gather(out_weight, "seq", axis=0, tiled=True),
        (((1,), (1,)), ((), ())),
        preferred_element_type=jnp.float32,
    ).astype(jnp.bfloat16)
    n_seq = lax.axis_size("seq")
    n_plasmid = lax.axis_size("dp")
    token_total = n_plasmid * n_seq * tok_rows
    local_term = lax.psum_scatter(
        lax.dot_general(
            attn, grad_out, (((0,), (0,)), ((), ())), preferred_element_type=jnp.float32
        ),
        "seq",
        scatter_dimension=0,
        tiled=True,
    )
    summed = lax.psum(local_term, "dp")
    weight_grad = summed * (1.0 / math.sqrt(token_total))
    dattn_soft = d_attn[:, :soft].reshape(tok_rows, SOFT_HEADS, DH)
    dprob = jnp.einsum("ihd,jhd->hij", dattn_soft, value_soft, preferred_element_type=jnp.float32)
    row_delta = jnp.sum(dattn_soft.astype(jnp.float32) * attn_soft.astype(jnp.float32), axis=2)
    dscore = (attn_probs * (dprob - row_delta.T[:, :, None])).astype(jnp.bfloat16)
    dq_soft = (
        jnp.einsum("hij,jhd->ihd", dscore, key_soft, preferred_element_type=jnp.float32) * factor
    )
    dk_span = (
        jnp.einsum("hij,ihd->jhd", dscore, query_soft, preferred_element_type=jnp.float32) * factor
    )
    dv_span = jnp.einsum("hij,ihd->jhd", probs_low, dattn_soft, preferred_element_type=jnp.float32)
    span_grads = jnp.stack([dk_span, dv_span]).reshape(2, span_rows, soft)
    from_next = from_behind(span_grads[:, :HALF], "seq", -1)
    from_prev = from_behind(span_grads[:, tok_rows + HALF :], "seq", 1)
    middle = span_grads[:, HALF : HALF + tok_rows]
    middle = middle + from_prev
    middle = middle + from_next
    lin_grad = gain_heads * d_attn[:, soft:].astype(jnp.float32).reshape(tok_rows, LIN_HEADS, DH)
    grad_u = lin_r * lin_grad - lin_u * lin_r**3 * jnp.mean(lin_grad * lin_u, axis=2, keepdims=True)
    dstate_term = jnp.einsum("iha,ihb->hab", phi_query, grad_u, precision=highest)
    dstate = lax.psum(dstate_term, "seq")
    dq_lin = jnp.einsum("ihb,hab->iha", grad_u, lin_state, precision=highest) * unit_slope(
        query_lin
    )
    dk_lin = jnp.einsum("jhb,hab->jha", value_lin, dstate, precision=highest) * unit_slope(key_lin)
    dv_lin = jnp.einsum("jha,hab->jhb", phi_key, dstate, precision=highest)
    lin_width = LIN_HEADS * DH
    query_grad = jnp.concatenate(
        [dq_soft.reshape(tok_rows, soft), dq_lin.reshape(tok_rows, lin_width)], axis=1
    ).astype(jnp.bfloat16)
    key_grad = jnp.concatenate([middle[0], dk_lin.reshape(tok_rows, lin_width)], axis=1).astype(
        jnp.bfloat16
    )
    value_grad = jnp.concatenate([middle[1], dv_lin.reshape(tok_rows, lin_width)], axis=1).astype(
        jnp.bfloat16
    )
    return (query_grad[None], key_grad[None], value_grad[None], weight_grad)


def solution(mesh):
    return jax.shard_map(
        body,
        mesh=mesh,
        in_specs=(
            P("dp", "seq", None),
            P("dp", "seq", None),
            P("dp", "seq", None),
            P("dp", "seq", None),
            P("seq", None),
            P(),
        ),
        out_specs=(
            P("dp", "seq", None),
            P("dp", "seq", None),
            P("dp", "seq", None),
            P("seq", None),
        ),
        check_vma=False,
    )
```

profile of v0, /device:TPU:8, one launch (start us, length us, event | category | flops | bytes accessed | tf_op | source)
XLA Modules:
  0.0 2277.1 jit_solution(10162035164895397284)
XLA Ops:
  7.2 0.0 all-gather.3.cloned.1.call-start
  7.2 0.7 all-gather.3.cloned.1.call-update
  7.9 0.0 all-reduce.5.cloned.1.call-start
  8.0 1.0 copy.67
  9.0 1.0 copy.68
  10.1 12.5 collective-permute-start.1
  22.6 1.9 collective-permute-start
  24.5 0.9 fusion.45
  25.4 0.0 all-reduce.5.cloned.1.call-update
  25.5 0.0 all-reduce.7.cloned.1.call-start
  25.5 1.0 copy.69
  26.7 6.4 collective-permute-done
  33.1 0.1 pad_maximum_fusion
  33.2 0.4 fusion.44
  33.5 196.6 %all-gather.3.cloned.1.call-done = bf16[128,4,1024]{2,1,0:T(4,128)(2,1)} async-done(((bf16[1,4,1024]{2,1,0:T(4,128)(2,1)}), bf16[128,4,1024]{2,1,0:T(4,128)(2,1)}) %all-gather.3.cloned.1.call-update) | async-done | bytes 1048592 | tf_op jit(solution)/shard_map/all_gather | solution.py:89
  230.1 1.3 reshape.183
  231.5 0.5 convolution_convert_fusion
  232.0 0.1 copy.114
  232.1 0.1 copy.113
  232.2 952.7 %all-reduce.5.cloned.1.call-done = f32[2,128,128]{2,1,0:T(8,128)} async-done(((f32[2,128,128]{2,1,0:T(8,128)}), f32[2,128,128]{2,1,0:T(8,128)}) %all-reduce.5.cloned.1.call-update) | async-done | bytes 131088 | tf_op jit(solution)/shard_map/psum | solution.py:79
  1184.9 1.3 multiply_reduce_fusion.1
  1186.2 0.1 multiply_convert_fusion
  1186.3 0.6 multiply_reduce_fusion.2
  1186.9 1.7 fusion.19
  1188.6 1.1 fusion.33
  1189.7 0.0 all-reduce.7.cloned.1.call-update
  1189.8 1.3 dynamic-slice
  1191.7 0.3 fusion.11
  1192.0 0.1 copy.84
  1192.2 0.3 fusion.8
  1192.4 0.2 fusion.3
  1192.6 0.2 copy.87
  1192.8 0.5 fusion.38
  1193.4 1.9 collective-permute-start.2
  1195.3 7.9 collective-permute-start.3
  1203.2 0.2 fusion.12
  1203.4 0.1 copy.83
  1203.5 0.7 pad_maximum_fusion.3
  1204.2 1.3 collective-permute-done.2
  1205.5 1.8 collective-permute-done.3
  1207.3 1038.3 %all-reduce.7.cloned.1.call-done = (f32[2,128,128]{2,1,0:T(8,128)}, f32[512,1024]{1,0:T(8,128)}) async-done(((f32[2,128,128]{2,1,0:T(8,128)}, f32[512,1024]{1,0:T(8,128)}), (f32[2,128,128]{2,1,0:T(8,128)}, f32[512,1024]{1,0:T(8,128)})) %all-reduce.7.cloned.1.call-update) | async-done | bytes 2228240 | tf_op jit(solution)/shard_map/psum | solution.py:126
  2245.6 1.3 convolution_convert_fusion.2
  2246.9 1.1 fusion.13
  2248.0 0.8 constant_dynamic-slice_fusion
  2248.8 19.6 psum.23
  2268.4 0.6 broadcast_multiply_fusion
  2269.1 0.8 copy.95
  2269.8 0.8 copy.94
  (23 shorter events, 0.4 us)
Async XLA Ops:
  7.2 224.3 %copy-start = (bf16[1,128,1024]{2,1,0:T(8,128)(2,1)S(1)}, bf16[1,128,1024]{2,1,0:T(8,128)(2,1)}, u32[]{:S(2)}) copy-start(bf16[1,128,1024]{2,1,0:T(8,128)(2,1)} %param.9) | copy-start | bytes 786436
  7.2 222.9 %all-gather.3.cloned.1.call-start = ((), (), s32[]{:S(2)}) async-start(), calls=%async_computation.1 | async-start | bytes 1056768 | tf_op jit(solution)/shard_map/all_gather | solution.py:89
  7.9 1177.0 %all-reduce.5.cloned.1.call-start = ((), (), s32[]{:S(2)}) async-start(), calls=%async_computation | async-start | bytes 262144 | tf_op jit(solution)/shard_map/psum | solution.py:79
  10.1 16.6 collective-permute-start.1
  22.6 10.5 collective-permute-start
  25.5 2220.1 %all-reduce.7.cloned.1.call-start = ((), (), s32[]{:S(2)}) async-start(), calls=%async_computation.2 | async-start | bytes 4456448 | tf_op jit(solution)/shard_map/psum | solution.py:126
  33.5 1151.3 %copy-start.2 = (f32[256]{0:T(256)S(1)}, f32[256]{0:T(256)}, u32[]{:S(2)}) copy-start(f32[256]{0:T(256)} %param.11) | copy-start | bytes 3076
  1186.9 4.8 copy-start.1
  1193.4 12.0 collective-permute-start.2
  1195.3 11.9 collective-permute-start.3
Sparse Core Ops, SparseCore 0:
  10.1 219.9 all-gather.2
  233.6 951.2 all-reduce.4
  1189.9 1055.7 all-reduce.6
where the time goes:
time: 2280 us
  waiting for transfers between devices  2200 us (96%)
  starting transfers between devices  24.3 us (1%)
    psum x1, waiting for transfers between devices, body(): dstate = lax.psum(dstate_term, 'seq')  1040 us
    psum x1, waiting for transfers between devices, body(): lin_state = lax.psum(state_term, 'seq')  953 us
    all_gather x1, waiting for transfers between devices, body(): lax.all_gather(out_weight, 'seq', axis=0, tiled=True)  197 us
  transfers between devices with their start and end apart: 7, of which 6 were waited for; matrix products, arithmetic and copies ran while one was open for 0% of the time, Pallas kernels for 0%

commit v1 on v0

--- a/solution.py
+++ b/solution.py
@@ -123,7 +123,7 @@
     lin_grad = gain_heads * d_attn[:, soft:].astype(jnp.float32).reshape(tok_rows, LIN_HEADS, DH)
     grad_u = lin_r * lin_grad - lin_u * lin_r**3 * jnp.mean(lin_grad * lin_u, axis=2, keepdims=True)
     dstate_term = jnp.einsum("iha,ihb->hab", phi_query, grad_u, precision=highest)
-    dstate = lax.psum(dstate_term, "seq")
+    dstate = jnp.sum(lax.all_gather(dstate_term, "seq"), axis=0)
     dq_lin = jnp.einsum("ihb,hab->iha", grad_u, lin_state, precision=highest) * unit_slope(
         query_lin
     )

time: 2280 us -> 2530 us (1.11)
  the two profiles are of different devices: /device:TPU:8 before, /device:TPU:1 now
where the time goes in v1:
time: 2530 us
  waiting for transfers between devices  2460 us (97%)
    unnamed x5, waiting for transfers between devices  1090 us
    psum x1, waiting for transfers between devices, body(): lin_state = lax.psum(state_term, 'seq')  950 us
    all_gather x1, waiting for transfers between devices, body(): dstate = jnp.sum(lax.all_gather(dstate_term, 'seq'), axis=0)  215 us
    all_gather x1, waiting for transfers between devices, body(): lax.all_gather(out_weight, 'seq', axis=0, tiled=True)  204 us
  transfers between devices with their start and end apart: 8, of which 6 were waited for; matrix products, arithmetic and copies ran while one was open for 1% of the time, Pallas kernels for 0%

profile of v1, /device:TPU:1, one launch (start us, length us, event | category | flops | bytes accessed | tf_op | source)
XLA Modules:
  0.0 2533.7 jit_solution(16657235458556284478)
XLA Ops:
  7.2 0.0 all-gather.7.cloned.1.call-start
  7.2 0.7 all-gather.7.cloned.1.call-update
  7.9 0.0 all-reduce.4.cloned.1.call-start
  8.0 1.0 copy.67
  9.0 1.0 copy.68
  10.1 8.7 collective-permute-start.1
  18.8 1.9 collective-permute-start
  20.8 0.9 fusion.45
  21.8 0.0 all-reduce.6.cloned.1.call-start
  21.8 1.0 copy.69
  23.0 4.9 collective-permute-done
  27.9 0.1 pad_maximum_fusion
  28.0 0.4 fusion.44
  28.4 203.8 %all-gather.7.cloned.1.call-done = bf16[128,4,1024]{2,1,0:T(4,128)(2,1)} async-done(((bf16[1,4,1024]{2,1,0:T(4,128)(2,1)}), bf16[128,4,1024]{2,1,0:T(4,128)(2,1)}) %all-gather.7.cloned.1.call-update) | async-done | bytes 1048592 | tf_op jit(solution)/shard_map/all_gather | solution.py:89
  232.2 1.3 reshape.184
  233.5 0.5 convolution_convert_fusion
  234.0 0.1 copy.114
  234.1 0.1 copy.113
  234.2 950.0 %all-reduce.4.cloned.1.call-done = f32[2,128,128]{2,1,0:T(8,128)} async-done(((f32[2,128,128]{2,1,0:T(8,128)}), f32[2,128,128]{2,1,0:T(8,128)}) %all-reduce.4.cloned.1.call-update) | async-done | bytes 131088 | tf_op jit(solution)/shard_map/psum | solution.py:79
  1184.2 1.3 multiply_reduce_fusion.1
  1185.5 0.1 multiply_convert_fusion
  1185.6 0.6 multiply_reduce_fusion.2
  1186.2 1.7 fusion.19
  1187.9 0.0 all-gather.5.cloned.1.call-start
  1188.0 1.1 fusion.33
  1189.1 1.3 dynamic-slice
  1191.1 0.3 fusion.11
  1191.4 0.1 copy.84
  1191.5 0.3 fusion.8
  1191.8 0.2 fusion.3
  1192.0 0.2 copy.87
  1192.2 0.5 fusion.38
  1192.8 1.9 collective-permute-start.2
  1194.7 3.6 collective-permute-start.3
  1198.3 0.2 fusion.12
  1198.5 0.1 copy.83
  1198.6 0.7 pad_maximum_fusion.3
  1199.3 3.3 collective-permute-done.3
  1202.7 1084.5 %all-reduce.6.cloned.1.call-done = f32[512,1024]{1,0:T(8,128)} async-done(((f32[512,1024]{1,0:T(8,128)}), f32[512,1024]{1,0:T(8,128)}) %all-reduce.6.cloned.1.call-update) | async-done | bytes 2097168
  2287.2 0.8 constant_dynamic-slice_fusion
  2287.9 15.0 psum.15
  2303.0 0.6 broadcast_multiply_fusion
  2303.6 214.8 %all-gather.5.cloned.1.call-done = f32[256,128,128]{2,1,0:T(8,128)} async-done(((f32[2,128,128]{2,1,0:T(8,128)}), f32[256,128,128]{2,1,0:T(8,128)}) %all-gather.5.cloned.1.call-update) | async-done | bytes 16777232 | tf_op jit(solution)/shard_map/all_gather | solution.py:126
  2518.4 6.6 reduce_sum.49
  2525.0 0.4 convolution_convert_fusion.2
  2525.4 0.2 fusion.13
  2525.6 0.8 copy.95
  2526.4 0.8 copy.94
  (27 shorter events, 0.4 us)
Async XLA Ops:
  7.2 226.3 %copy-start = (bf16[1,128,1024]{2,1,0:T(8,128)(2,1)S(1)}, bf16[1,128,1024]{2,1,0:T(8,128)(2,1)}, u32[]{:S(2)}) copy-start(bf16[1,128,1024]{2,1,0:T(8,128)(2,1)} %param.9) | copy-start | bytes 786436
  7.2 225.0 %all-gather.7.cloned.1.call-start = ((), (), s32[]{:S(2)}) async-start(), calls=%async_computation.2 | async-start | bytes 1056768 | tf_op jit(solution)/shard_map/all_gather | solution.py:89
  7.9 1176.3 %all-reduce.4.cloned.1.call-start = ((), (), s32[]{:S(2)}) async-start(), calls=%async_computation | async-start | bytes 262144 | tf_op jit(solution)/shard_map/psum | solution.py:79
  10.1 12.9 collective-permute-start.1
  18.8 9.1 collective-permute-start
  21.8 2265.4 %all-reduce.6.cloned.1.call-start = ((), (), s32[]{:S(2)}) async-start(), calls=%async_computation.3 | async-start | bytes 4194304
  28.4 1155.8 %copy-start.2 = (f32[256]{0:T(256)S(1)}, f32[256]{0:T(256)}, u32[]{:S(2)}) copy-start(f32[256]{0:T(256)} %param.11) | copy-start | bytes 3076
  1186.2 4.9 copy-start.1
  1187.9 1330.5 %all-gather.5.cloned.1.call-start = ((), (), s32[]{:S(2)}) async-start(), calls=%async_computation.1 | async-start | bytes 16908288 | tf_op jit(solution)/shard_map/all_gather | solution.py:126
  1192.8 6.5 collective-permute-start.2
  1194.7 7.9 collective-permute-start.3
Sparse Core Ops, SparseCore 0:
  10.1 221.9 all-gather.6
  235.6 948.5 all-reduce.3
  1188.1 1099.0 all-reduce.5
  2289.8 228.5 all-gather.4
